TPU v7x, 256 devices: a whole 4x4x8 slice. The times are simulated.
256 devices in a mesh: row: 8 (over z_lo, core), col: 16 (over y, x), samp: 2 (over z_hi).
Axes of the slice: x: 4, y: 4, z: 8 (z_hi: 2, z_lo: 4; z = z_hi * 4 + z_lo), core: 2. Of those that a mesh axis runs over, the one named last changes fastest.
Arguments:
- pair_in: bfloat16 [512, 512, 128], P('row', 'col'), may hold values from -6 to 6
- residue_index: int32 [512], replicated, may hold values from 0 to 47
- chain_index: int32 [512], replicated, may hold values from 0 to 2
- token_mask: int32 [512], replicated, may hold values 0 or 1
- relpos_weight: bfloat16 [66, 128], replicated, may hold values from -5 to 5
- tri_proj: bfloat16 [128, 640], replicated, may hold values from -0.5 to 0.5
- tri_out: bfloat16 [128, 128], replicated, may hold values from -0.5 to 0.5
- bias_proj: bfloat16 [128, 16], replicated, may hold values from -0.5 to 0.5
- single: bfloat16 [512, 384], P('row'), may hold values from -6 to 6
- ada_proj: bfloat16 [384, 2304], replicated, may hold values from -0.3125 to 0.3125
- noisy: bfloat16 [16, 512, 768], P('samp', 'row'), may hold values from -6 to 6
- qkv_proj: bfloat16 [768, 3, 768], P(None, None, 'col'), may hold values from -0.21875 to 0.21875
- out_proj: bfloat16 [768, 768], P('col'), may hold values from -0.21875 to 0.21875
- cotangent: bfloat16 [16, 512, 768], P('samp', 'row', 'col'), may hold values from -6 to 6
Outputs:
- pair_out: bfloat16 [512, 512, 128], P('row', 'col')
- block_out: bfloat16 [16, 512, 768], P('samp', 'row', 'col')
- grad_pair: float32 [512, 512, 128], P('row', 'col')
- grad_single: float32 [512, 384], P('row')
All inputs are finite; a program needn't handle non-finite values.
Results may differ from a plain program's by a relative error of at most 0.012.
The roundings to bfloat16 on the way count: a program that leaves them out, or rounds other values in their place, can miss the bound.
Values may be sent and summed in bfloat16 or wider, within the bound.
A program may use at most 128 MiB of HBM per device.

v0:
```python
import jax
import jax.numpy as jnp
from jax import lax
from jax.sharding import PartitionSpec as P

HEAD_DIM = 48
REL_BINS = 66
EPSILON = 1e-05
HIGHEST = lax.Precision.HIGHEST


def joined_along(blocks, dim):
    dims = list(blocks.shape[1:])
    dims[dim] *= blocks.shape[0]
    return jnp.moveaxis(blocks, 0, dim).reshape(dims)


def sent_to_all(array, axis):
    copies = jnp.broadcast_to(array, (lax.axis_size(axis), *array.shape))
    return lax.all_to_all(copies, axis, split_axis=0, concat_axis=0, tiled=True)


def collect(array, axis, dim):
    return joined_along(sent_to_all(array, axis), dim)


def split_up(array, dim, size):
    dims = array.shape
    blocks = array.reshape(*dims[:dim], size, dims[dim] // size, *dims[dim + 1 :])
    return jnp.moveaxis(blocks, dim, 0)


def sent_and_summed(array, axis, dim):
    size = lax.axis_size(axis)
    blocks = lax.all_to_all(split_up(array, dim, size), axis, 0, 0, tiled=True)
    return jnp.sum(blocks, axis=0)


def gathered_total(array, axis):
    return lax.all_gather(array, axis).sum(0)


def taken_together(array, axis):
    return sent_to_all(array, axis).sum(axis=0)


def normalize(values_in):
    average = jnp.mean(values_in, -1, keepdims=True)
    centered = values_in - average
    variance = jnp.mean(centered * centered, -1, keepdims=True)
    return centered * lax.rsqrt(variance + EPSILON)


def normalize_grad(values_in, upstream):
    average = jnp.mean(values_in, -1, keepdims=True)
    centered = values_in - average
    variance = jnp.mean(centered * centered, -1, keepdims=True)
    inv_std = lax.rsqrt(variance + EPSILON)
    unit_rows = centered * inv_std
    return inv_std * (
        upstream
        - jnp.mean(upstream, -1, keepdims=True)
        - unit_rows * jnp.mean(upstream * unit_rows, -1, keepdims=True)
    )


def relative_embedding(res_rows, res_cols, chain_rows, chain_cols, relpos_weight):
    max_offset = (REL_BINS - 2) // 2
    offset = res_rows[:, None] - res_cols[None, :]
    bucket = jnp.where(
        chain_rows[:, None] == chain_cols[None, :],
        jnp.clip(offset + max_offset, 0, 2 * max_offset),
        REL_BINS - 1,
    )
    onehot = (bucket[:, :, None] == jnp.arange(REL_BINS, dtype=jnp.int32)[None, None, :]).astype(
        jnp.bfloat16
    )
    return jnp.einsum("ijr,rc->ijc", onehot, relpos_weight, preferred_element_type=jnp.float32)


def on_device(
    pair_in,
    residue_index,
    chain_index,
    token_mask,
    relpos_weight,
    tri_proj,
    tri_out,
    bias_proj,
    single,
    ada_proj,
    noisy,
    qkv_proj,
    out_proj,
    cotangent,
):
    tile_rows, tile_cols, pair_width = pair_in.shape
    row_at = lax.axis_index("row") * tile_rows
    col_at = lax.axis_index("col") * tile_cols
    res_rows = lax.dynamic_slice_in_dim(residue_index, row_at, tile_rows)
    res_cols = lax.dynamic_slice_in_dim(residue_index, col_at, tile_cols)
    chain_rows = lax.dynamic_slice_in_dim(chain_index, row_at, tile_rows)
    chain_cols = lax.dynamic_slice_in_dim(chain_index, col_at, tile_cols)
    pair_full = pair_in.astype(jnp.float32) + relative_embedding(
        res_rows, res_cols, chain_rows, chain_cols, relpos_weight
    )
    normed_pair = normalize(pair_full).astype(jnp.bfloat16)
    projected = jnp.dot(normed_pair, tri_proj, preferred_element_type=jnp.float32)
    mask_f = token_mask.astype(jnp.float32)
    mask_rows = lax.dynamic_slice_in_dim(mask_f, row_at, tile_rows)
    mask_cols = lax.dynamic_slice_in_dim(mask_f, col_at, tile_cols)
    pair_mask = (mask_rows[:, None] * mask_cols[None, :])[:, :, None]
    left_side = (
        jax.nn.sigmoid(projected[..., pair_width : 2 * pair_width])
        * projected[..., :pair_width]
        * pair_mask
    ).astype(jnp.bfloat16)
    right_side = (
        jax.nn.sigmoid(projected[..., 3 * pair_width : 4 * pair_width])
        * projected[..., 2 * pair_width : 3 * pair_width]
        * pair_mask
    ).astype(jnp.bfloat16)
    tri_gate = jax.nn.sigmoid(projected[..., 4 * pair_width :])
    right_all = lax.all_gather(right_side, "row", axis=0, tiled=True)
    triangle = jnp.swapaxes(
        lax.psum_scatter(
            jnp.einsum("jkc,ikc->jic", right_all, left_side, preferred_element_type=jnp.float32),
            "col",
            scatter_dimension=0,
            tiled=True,
        ),
        0,
        1,
    )
    update = jnp.dot(
        normalize(triangle).astype(jnp.bfloat16), tri_out, preferred_element_type=jnp.float32
    )
    pair_out = (pair_full + tri_gate * update).astype(jnp.bfloat16)
    head_count = qkv_proj.shape[2] // HEAD_DIM
    tile_bias = jnp.einsum(
        "ijc,ch->hij", pair_out, bias_proj, preferred_element_type=jnp.float32
    ).astype(jnp.bfloat16)
    head_bias = lax.all_to_all(tile_bias, "col", split_axis=0, concat_axis=2, tiled=True)
    model_width = noisy.shape[2]
    sample_count, tokens_here = (noisy.shape[0], noisy.shape[1])
    inner_width = qkv_proj.shape[2]
    cvec = normalize(single.astype(jnp.float32)).astype(jnp.bfloat16)
    conditioning = jnp.dot(cvec, ada_proj, preferred_element_type=jnp.float32)
    ada_scale = jax.nn.sigmoid(conditioning[:, :model_width])
    ada_shift = conditioning[:, model_width : 2 * model_width]
    out_gate = jax.nn.sigmoid(conditioning[:, 2 * model_width :])
    normed_in = normalize(noisy.astype(jnp.float32))
    hidden = (ada_scale * normed_in + ada_shift).astype(jnp.bfloat16)
    qkv_all = jnp.einsum(
        "std,dqe->stqe", hidden, qkv_proj, preferred_element_type=jnp.float32
    ).astype(jnp.bfloat16)
    keyval = collect(qkv_all[:, :, 1:], "row", 1)
    key_count = keyval.shape[1]
    queries = qkv_all[:, :, 0].reshape(sample_count, tokens_here, head_count, HEAD_DIM)
    key_rows = keyval[:, :, 0].reshape(sample_count, key_count, head_count, HEAD_DIM)
    value_rows = keyval[:, :, 1].reshape(sample_count, key_count, head_count, HEAD_DIM)
    score_scale = 1.0 / HEAD_DIM**0.5
    key_ok = token_mask > 0
    scores = (
        jnp.einsum("sihd,sjhd->shij", queries, key_rows, preferred_element_type=jnp.float32)
        * score_scale
    )
    scores = scores + head_bias.astype(jnp.float32)[None]
    scores = jnp.where(key_ok[None, None, None, :], scores, -1000000000.0)
    probs = jax.nn.softmax(scores, axis=-1)
    probs_b = probs.astype(jnp.bfloat16)
    attended = jnp.einsum(
        "shij,sjhd->sihd", probs_b, value_rows, preferred_element_type=jnp.float32
    ).astype(jnp.bfloat16)
    attended = attended.reshape(sample_count, tokens_here, inner_width)
    mixed_part = jnp.einsum("ste,ed->std", attended, out_proj, preferred_element_type=jnp.float32)
    mixed = sent_and_summed(mixed_part, "col", 2)
    feature_block = mixed.shape[2]
    feat_at = lax.axis_index("col") * feature_block
    gate_block = lax.dynamic_slice_in_dim(out_gate, feat_at, feature_block, 1)
    noisy_block = lax.dynamic_slice_in_dim(noisy, feat_at, feature_block, 2)
    block_out = (noisy_block.astype(jnp.float32) + gate_block * mixed).astype(jnp.bfloat16)
    grad_in = cotangent.astype(jnp.float32)
    d_mixed = (grad_in * gate_block).astype(jnp.bfloat16)
    d_gate = jnp.sum(grad_in * mixed, 0) * gate_block * (1.0 - gate_block)
    d_att = jnp.einsum(
        "std,ed->ste", collect(d_mixed, "col", 2), out_proj, preferred_element_type=jnp.float32
    )
    d_att = d_att.astype(jnp.bfloat16).reshape(sample_count, tokens_here, head_count, HEAD_DIM)
    d_probs = jnp.einsum("sihd,sjhd->shij", d_att, value_rows, preferred_element_type=jnp.float32)
    d_scores = probs * (d_probs - jnp.sum(probs * d_probs, -1, keepdims=True))
    d_scaled = (d_scores * score_scale).astype(jnp.bfloat16)
    d_query = jnp.einsum(
        "shij,sjhd->sihd", d_scaled, key_rows, preferred_element_type=jnp.float32
    ).astype(jnp.bfloat16)
    d_keys = jnp.einsum("shij,sihd->sjhd", d_scaled, queries, preferred_element_type=jnp.float32)
    d_values = jnp.einsum("shij,sihd->sjhd", probs_b, d_att, preferred_element_type=jnp.float32)
    d_keyval = jnp.stack(
        [
            d_keys.reshape(sample_count, key_count, inner_width),
            d_values.reshape(sample_count, key_count, inner_width),
        ],
        2,
    )
    d_keyval = sent_and_summed(d_keyval, "row", 1).astype(jnp.bfloat16)
    d_qkv = jnp.concatenate([d_query, d_keyval], 2)
    d_hidden = jnp.einsum("stqe,dqe->std", d_qkv, qkv_proj, preferred_element_type=jnp.float32)
    d_scale = jnp.sum(d_hidden * normed_in, 0)
    d_shift = jnp.sum(d_hidden, 0)
    w_ada = ada_proj.astype(jnp.float32)
    w_gate = lax.dynamic_slice_in_dim(w_ada, 2 * model_width + feat_at, feature_block, 1)
    d_cvec = jnp.dot(
        d_scale * ada_scale * (1.0 - ada_scale), w_ada[:, :model_width].T, precision=HIGHEST
    )
    d_cvec = d_cvec + jnp.dot(d_shift, w_ada[:, model_width : 2 * model_width].T, precision=HIGHEST)
    d_cvec = d_cvec + jnp.dot(d_gate, w_gate.T, precision=HIGHEST)
    d_cvec = gathered_total(d_cvec, ("col", "samp"))
    grad_single = normalize_grad(single.astype(jnp.float32), d_cvec)
    d_bias = jnp.sum(d_scores, 0)
    d_bias = taken_together(d_bias, "samp")
    d_tile = lax.all_to_all(d_bias, "col", split_axis=2, concat_axis=0, tiled=True)
    grad_pair = jnp.einsum("hij,ch->ijc", d_tile, bias_proj.astype(jnp.float32), precision=HIGHEST)
    return (pair_out, block_out, grad_pair, grad_single)


def solution(mesh):
    return jax.shard_map(
        on_device,
        mesh=mesh,
        in_specs=(
            P("row", "col", None),
            P(),
            P(),
            P(),
            P(),
            P(),
            P(),
            P(),
            P("row", None),
            P(),
            P("samp", "row", None),
            P(None, None, "col"),
            P("col", None),
            P("samp", "row", "col"),
        ),
        out_specs=(
            P("row", "col", None),
            P("samp", "row", "col"),
            P("row", "col", None),
            P("row", None),
        ),
        check_vma=False,
    )
```

profile of v0, /device:TPU:32, one launch (start us, length us, event | category | flops | bytes accessed | tf_op | source)
XLA Modules:
  0.0 503.7 jit_solution(2397835421734303942)
XLA Ops:
  11.2 1.8 fusion.118
  15.2 1.8 fusion.22
  17.7 1.7 copy.132
  19.5 51.6 %all-gather.4.cloned.1.call-done = bf16[512,32,128]{2,1,0:T(8,128)(2,1)} async-done(((bf16[64,32,128]{2,1,0:T(8,128)(2,1)}), bf16[512,32,128]{2,1,0:T(8,128)(2,1)}) %all-gather.4.cloned.1.call-update) | async-done | bytes 4194320 | tf_op jit(solution)/shard_map/all_gather | solution.py:124
  71.0 8.6 %copy.133 = bf16[512,32,128]{0,1,2:T(8,128)(2,1)} copy(bf16[512,32,128]{2,1,0:T(8,128)(2,1)} %all-gather.4.cloned.1.call-done) | data formatting | bytes 8388608 | tf_op jit(solution)/shard_map/all_gather | solution.py:124
  79.7 10.3 %convolution_bitcast_fusion = f32[512,64,128]{0,1,2:T(8,128)} fusion(bf16[64,32,128]{0,1,2:T(8,128)(2,1)S(1)} %copy.132, bf16[512,32,128]{0,1,2:T(8,128)(2,1)} %copy.133), kind=kOutput, calls=%fused_computation.2 | convolution fusion | flops 268435456 | bytes 21495808 | tf_op jit(solution)/shard_map/jkc,ikc->jic/dot_general | solution.py:127
  89.9 16.8 %copy.134 = f32[512,64,128]{2,1,0:T(8,128)} copy(f32[512,64,128]{0,1,2:T(8,128)} %convolution_bitcast_fusion) | data formatting | bytes 33554432 | tf_op jit(solution)/shard_map/jkc,ikc->jic/transpose | solution.py:127
  108.5 2.0 fusion.82
  113.8 2.0 reshape.267
  115.8 9.1 %all-to-all-start = ((bf16[8,2,24576]{2,1,0:T(2,128)(2,1)}), bf16[8,2,24576]{2,1,0:T(2,128)(2,1)}, u32[]{:S(2)}, u32[]{:S(2)}) async-start(bf16[8,2,24576]{2,1,0:T(2,128)(2,1)} %reshape.267), calls=%async_computation.1 | async-start | bytes 1572864 | tf_op jit(solution)/shard_map/all_to_all | solution.py:20
  125.1 17.2 %all-to-all-done = bf16[8,2,24576]{2,1,0:T(2,128)(2,1)} async-done(((bf16[8,2,24576]{2,1,0:T(2,128)(2,1)}), bf16[8,2,24576]{2,1,0:T(2,128)(2,1)}, u32[]{:S(2)}, u32[]{:S(2)}) %all-to-all-start) | async-done | bytes 786464 | tf_op jit(solution)/shard_map/all_to_all | solution.py:20
  142.4 2.2 reshape.268
  144.6 80.7 %reduce-scatter.2.cloned.1.call-done = f32[32,64,128]{2,1,0:T(8,128)} async-done(((f32[512,64,128]{2,1,0:T(8,128)}), f32[32,64,128]{2,1,0:T(8,128)}) %reduce-scatter.2.cloned.1.call-update) | async-done | bytes 1048592 | tf_op jit(solution)/shard_map/reduce_scatter | solution.py:126
  225.3 1.7 bitcast_reduce_fusion.1
  228.3 1.8 fusion.17
  232.8 4.8 all-to-all-start.1
  239.7 5.5 %all-to-all-done.1 = bf16[16,2,1024]{2,1,0:T(2,128)(2,1)S(1)} async-done(((bf16[16,2,1024]{2,1,0:T(2,128)(2,1)}), bf16[16,2,1024]{2,1,0:T(2,128)(2,1)S(1)}, u32[]{:S(2)}, u32[]{:S(2)}) %all-to-all-start.1) | async-done | bytes 65568 | tf_op jit(solution)/shard_map/all_to_all | solution.py:143
  245.6 1.5 fusion.119
  248.1 2.5 convolution_bitcast_fusion.1
  250.6 2.2 copy.172
  252.8 2.9 reshape.271
  255.7 3.9 all-to-all-start.2
  262.4 19.4 %all-to-all-done.2 = f32[16,1,24576]{2,1,0:T(1,128)S(1)} async-done(((f32[16,1,24576]{2,1,0:T(1,128)}), f32[16,1,24576]{2,1,0:T(1,128)S(1)}, u32[]{:S(2)}, u32[]{:S(2)}) %all-to-all-start.2) | async-done | bytes 1572896 | tf_op jit(solution)/shard_map/all_to_all | solution.py:35
  282.3 6.2 %reduce.12 = f32[16,24576]{1,0:T(8,128)} reduce(f32[16,1,24576]{2,1,0:T(1,128)S(1)} %all-to-all-done.2, f32[]{:T(128)} %broadcast.247), dimensions={1}, to_apply=%all_to_all.37.reduce_sub_computation | reduce | bytes 3145732 | tf_op jit(solution)/shard_map/all_to_all | solution.py:35
  288.5 2.4 reshape.272
  291.8 1.3 fusion.62
  294.7 16.6 %all_to_all.52 = bf16[16,2,12288]{2,1,0:T(2,128)(2,1)S(1)} all-to-all(bf16[16,2,12288]{2,1,0:T(2,128)(2,1)S(1)} %reshape.273), channel_id=1, replica_groups=mesh['row'=8,'col'=16,'samp'=2] {'col'}, dimensions={0} | all-to-all | bytes 1572864 | tf_op jit(solution)/shard_map/all_to_all | solution.py:20
  313.5 3.5 copy.144
  317.1 2.5 reshape.251
  320.1 1.3 fusion.51
  322.4 4.4 convolution_bitcast_fusion.3
  326.8 2.6 pad_maximum_fusion
  329.3 2.4 reshape.252
  331.8 2.2 copy.171
  334.0 4.8 reshape.277
  338.8 5.5 %all-to-all-start.6 = ((f32[8,1,49152]{2,1,0:T(1,128)}), f32[8,1,49152]{2,1,0:T(1,128)S(1)}, u32[]{:S(2)}, u32[]{:S(2)}) async-start(f32[8,1,49152]{2,1,0:T(1,128)} %reshape.277), calls=%async_computation.7 | async-start | bytes 3145728 | tf_op jit(solution)/shard_map/all_to_all | solution.py:35
  344.6 5.4 %fusion.20 = bf16[8,64,1,48]{1,3,2,0:T(8,128)(2,1)} fusion(bf16[8,512,2,48]{1,3,0,2:T(8,128)(2,1)S(1)} %copy-done.8, f32[8,64,512]{2,1,0:T(8,128)} %copy-done.11, f32[8,64,512]{2,1,0:T(8,128)} %copy-done.13, f32[8,64]{1,0:T(8,128)S(1)} %copy-done.33), kind=kOutput, calls=%fused_computation.37 | convolution fusion | flops 27026432 | bytes 4644864 | tf_op jit(solution)/shard_map/shij,sjhd->sihd/dot_general | solution.py:193
  350.1 28.6 %all-to-all-done.6 = f32[8,1,49152]{2,1,0:T(1,128)S(1)} async-done(((f32[8,1,49152]{2,1,0:T(1,128)}), f32[8,1,49152]{2,1,0:T(1,128)S(1)}, u32[]{:S(2)}, u32[]{:S(2)}) %all-to-all-start.6) | async-done | bytes 1572896 | tf_op jit(solution)/shard_map/all_to_all | solution.py:35
  378.7 6.3 %reduce.15 = f32[8,49152]{1,0:T(8,128)} reduce(f32[8,1,49152]{2,1,0:T(1,128)S(1)} %all-to-all-done.6, f32[]{:T(128)} %broadcast.247), dimensions={1}, to_apply=%all_to_all.44.reduce_sub_computation | reduce | bytes 3145732 | tf_op jit(solution)/shard_map/all_to_all | solution.py:35
  384.9 2.7 reshape.278
  390.2 1.6 fusion.42
  393.5 2.8 fusion.120
  396.3 14.8 %all_to_all.53 = f32[2,1,64,512]{3,2,1,0:T(8,128)S(1)} all-to-all(f32[2,1,64,512]{3,2,1,0:T(8,128)S(1)} %broadcast_in_dim.23), channel_id=1, replica_groups=mesh['row'=8,'col'=16,'samp'=2] {'samp'}, dimensions={0} | all-to-all | bytes 524288 | tf_op jit(solution)/shard_map/all_to_all | solution.py:20
  411.3 1.3 reduce.13
  412.8 11.2 %all_to_all.54 = f32[16,1,2048]{2,1,0:T(1,128)S(1)} all-to-all(f32[16,1,2048]{2,1,0:T(1,128)S(1)} %reshape.275), channel_id=1, replica_groups=mesh['row'=8,'col'=16,'samp'=2] {'col'}, dimensions={0} | all-to-all | bytes 262144 | tf_op jit(solution)/shard_map/all_to_all | solution.py:221
  425.7 2.0 fusion.45
  427.7 65.2 %all-gather.6.cloned.1.call-done = f32[2048,384]{1,0:T(8,128)} async-done(((f32[64,384]{1,0:T(8,128)}), f32[2048,384]{1,0:T(8,128)}) %all-gather.6.cloned.1.call-update) | async-done | bytes 3145744 | tf_op jit(solution)/shard_map/all_gather | solution.py:40
  492.9 2.2 reduce_sum.208
  (152 shorter events, 37.0 us)
Async XLA Ops:
  7.2 104.9 %copy-start = (bf16[768,3,48]{0,2,1:T(8,128)(2,1)S(1)}, bf16[768,3,48]{0,2,1:T(8,128)(2,1)}, u32[]{:S(2)}) copy-start(bf16[768,3,48]{0,2,1:T(8,128)(2,1)} %param.25) | copy-start | bytes 663556
  7.2 6.9 %copy-start.19 = (bf16[128,640]{1,0:T(8,128)(2,1)S(1)}, bf16[128,640]{1,0:T(8,128)(2,1)}, u32[]{:S(2)}) copy-start(bf16[128,640]{1,0:T(8,128)(2,1)} %param.19) | copy-start | bytes 491524
  7.2 63.8 %all-gather.4.cloned.1.call-start = ((), (), s32[]{:S(2)}) async-start(), calls=%async_computation.8 | async-start | bytes 4718592 | tf_op jit(solution)/shard_map/all_gather | solution.py:124
  15.1 2.6 copy-start.1
  17.7 207.6 %reduce-scatter.2.cloned.1.call-start = ((), (), s32[]{:S(2)}) async-start(), calls=%async_computation.9 | async-start | bytes 17825792 | tf_op jit(solution)/shard_map/reduce_scatter | solution.py:126
  106.7 0.8 copy-start.10
  106.7 1.2 copy-start.4
  107.7 2.8 copy-start.25
  108.5 3.6 copy-start.28
  108.5 3.6 copy-start.30
  110.5 0.8 copy-start.9
  112.8 0.7 copy-start.20
  113.8 11.1 %copy-start.17 = (bf16[48,768]{1,0:T(8,128)(2,1)S(1)}, bf16[48,768]{1,0:T(8,128)(2,1)}, u32[]{:S(2)}) copy-start(bf16[48,768]{1,0:T(8,128)(2,1)} %param.26) | copy-start | bytes 221188
  113.8 11.3 %copy-start.27 = (s32[512]{0:T(512)S(1)}, s32[512]{0:T(512)}, u32[]{:S(2)}) copy-start(s32[512]{0:T(512)} %param.17) | copy-start | bytes 6148
  115.8 26.6 %all-to-all-start = ((bf16[8,2,24576]{2,1,0:T(2,128)(2,1)}), bf16[8,2,24576]{2,1,0:T(2,128)(2,1)}, u32[]{:S(2)}, u32[]{:S(2)}) async-start(bf16[8,2,24576]{2,1,0:T(2,128)(2,1)} %reshape.267), calls=%async_computation.1 | async-start | bytes 1572864 | tf_op jit(solution)/shard_map/all_to_all | solution.py:20
  225.3 1.7 copy-start.3
  226.9 1.3 copy-start.34
  228.3 2.7 copy-start.24
  230.1 0.8 copy-start.16
  232.8 12.5 %all-to-all-start.1 = ((bf16[16,2,1024]{2,1,0:T(2,128)(2,1)}), bf16[16,2,1024]{2,1,0:T(2,128)(2,1)S(1)}, u32[]{:S(2)}, u32[]{:S(2)}) async-start(bf16[16,2,1024]{2,1,0:T(2,128)(2,1)} %reshape.269), calls=%async_computation.2 | async-start | bytes 131072 | tf_op jit(solution)/shard_map/all_to_all | solution.py:143
  239.7 7.3 %copy-start.7 = (bf16[8,512,2,48]{1,3,0,2:T(8,128)(2,1)}, bf16[8,512,2,48]{1,3,0,2:T(8,128)(2,1)S(1)}, u32[]{:S(2)}) copy-start(bf16[8,512,2,48]{1,3,0,2:T(8,128)(2,1)S(1)} %reshape.246) | copy-start | bytes 2359300
  247.1 1.0 copy-start.13
  247.1 1.0 copy-start.32
  255.7 26.1 %all-to-all-start.2 = ((f32[16,1,24576]{2,1,0:T(1,128)}), f32[16,1,24576]{2,1,0:T(1,128)S(1)}, u32[]{:S(2)}, u32[]{:S(2)}) async-start(f32[16,1,24576]{2,1,0:T(1,128)} %reshape.271), calls=%async_computation.3 | async-start | bytes 3145728 | tf_op jit(solution)/shard_map/all_to_all | solution.py:35
  290.9 0.7 copy-start.22
  290.9 0.9 copy-start.23
  317.1 2.5 copy-start.18
  319.5 1.9 copy-start.14
  319.6 1.9 copy-start.33
  321.4 1.0 copy-start.11
  338.8 5.7 %copy-start.21 = (f32[64,48]{0,1:T(8,128)S(1)}, f32[64,48]{0,1:T(8,128)}, u32[]{:S(2)}) copy-start(f32[64,48]{0,1:T(8,128)} %get-tuple-element.11) | copy-start | bytes 36868
  338.8 5.8 %copy-start.8 = (bf16[8,512,2,48]{1,3,0,2:T(8,128)(2,1)S(1)}, bf16[8,512,2,48]{1,3,0,2:T(8,128)(2,1)}, u32[]{:S(2)}) copy-start(bf16[8,512,2,48]{1,3,0,2:T(8,128)(2,1)} %copy-done.7) | copy-start | bytes 2359300
  338.8 39.8 %all-to-all-start.6 = ((f32[8,1,49152]{2,1,0:T(1,128)}), f32[8,1,49152]{2,1,0:T(1,128)S(1)}, u32[]{:S(2)}, u32[]{:S(2)}) async-start(f32[8,1,49152]{2,1,0:T(1,128)} %reshape.277), calls=%async_computation.7 | async-start | bytes 3145728 | tf_op jit(solution)/shard_map/all_to_all | solution.py:35
  344.3 148.6 %all-gather.6.cloned.1.call-start = ((), (), s32[]{:S(2)}) async-start(), calls=%async_computation.10 | async-start | bytes 3244032 | tf_op jit(solution)/shard_map/all_gather | solution.py:40
  387.6 1.1 copy-start.5
  387.6 1.1 copy-start.31
  387.6 1.1 copy-start.35
  388.7 1.5 copy-start.6
  389.3 4.2 copy-start.12
  389.3 4.2 copy-start.15
  492.9 2.2 copy-start.26
  492.9 2.2 copy-start.29
  492.9 2.8 copy-start.2
Sparse Core Ops, SparseCore 0:
  17.8 53.1 all-gather.3
  106.9 118.3 reduce-scatter.1
  393.6 99.2 all-gather.5
where the time goes:
time: 513 us; the launch traced here: 504 us
  waiting for transfers between devices  268 us (52%)
  local copies, waits for them, and re-layouts  80 us (16%)
  blocking collectives  42.6 us (8%)
  matrix products  40.2 us (8%)
  other arithmetic  34.2 us (7%)
  starting transfers between devices  23.6 us (5%)
  between operations  14.8 us (3%)
    reduce_scatter x1, waiting for transfers between devices, on_device(): lax.psum_scatter(jnp.einsum('jkc,ikc->jic', right_all, left_side, preferr...  80.7 us
    all_gather x1, waiting for transfers between devices, gathered_total(): return lax.all_gather(array, axis).sum(0)  65.2 us
    all_gather x1, waiting for transfers between devices, on_device(): right_all = lax.all_gather(right_side, 'row', axis=0, tiled=True)  51.6 us
    all_to_all x2, waiting for transfers between devices, sent_and_summed(): blocks = lax.all_to_all(split_up(array, dim, size), axis, 0, 0, tiled=True)  47.9 us
    all_to_all x2, blocking collectives, sent_to_all(): return lax.all_to_all(copies, axis, split_axis=0, concat_axis=0, tiled=True)  31.4 us
    unnamed x87, local copies, waits for them, and re-layouts  29.6 us
    all_to_all x1, waiting for transfers between devices, sent_to_all(): return lax.all_to_all(copies, axis, split_axis=0, concat_axis=0, tiled=True)  17.2 us
    transpose x1, local copies, waits for them, and re-layouts, on_device(): jnp.einsum('jkc,ikc->jic', right_all, left_side, preferred_element_type=j...  16.8 us
  transfers between devices with their start and end apart: 7, of which 7 were waited for; matrix products, arithmetic and copies ran while one was open for 6% of the time, Pallas kernels for 0%

commit v1 on v0

--- a/solution.py
+++ b/solution.py
@@ -121,7 +121,8 @@
         * pair_mask
     ).astype(jnp.bfloat16)
     tri_gate = jax.nn.sigmoid(projected[..., 4 * pair_width :])
-    right_all = lax.all_gather(right_side, "row", axis=0, tiled=True)
+    repeated = jnp.stack([right_side] * lax.axis_size("row"))
+    right_all = jnp.concatenate(lax.all_to_all(repeated, "row", 0, 0), axis=0)
     triangle = jnp.swapaxes(
         lax.psum_scatter(
             jnp.einsum("jkc,ikc->jic", right_all, left_side, preferred_element_type=jnp.float32),

time: 513 us -> 562 us (1.096)
  waiting for transfers between devices: 268 us -> 308 us
    all_to_all x0 -> x1, waiting for transfers between devices: none -> 88.8 us  [on_device(): right_all = jnp.concatenate(lax.all_to_all(repeated, 'row', 0, 0), axis=0)]
    all_gather x1 -> x0, waiting for transfers between devices: 51.6 us -> none  [on_device(): right_all = lax.all_gather(right_side, 'row', axis=0, tiled=True)]
    all_gather x1 -> x0, local copies, waits for them, and re-layouts: 8.64 us -> none  [on_device(): right_all = lax.all_gather(right_side, 'row', axis=0, tiled=True)]
    reshape x0 -> x1, local copies, waits for them, and re-layouts: none -> 8.6 us  [on_device(): right_all = jnp.concatenate(lax.all_to_all(repeated, 'row', 0, 0), axis=0)]
    all_to_all x0 -> x1, starting transfers between devices: none -> 6.24 us  [on_device(): right_all = jnp.concatenate(lax.all_to_all(repeated, 'row', 0, 0), axis=0)]
  transfers between devices with their start and end apart: 7 -> 7, of which waited for: 7 -> 7; matrix products, arithmetic and copies ran while one was open for 6% -> 5% of each run, Pallas kernels for 0% -> 0%
where the time goes in v1:
time: 562 us; the launch traced here: 552 us
  waiting for transfers between devices  308 us (55%)
  local copies, waits for them, and re-layouts  83.7 us (15%)
  blocking collectives  42.7 us (8%)
  matrix products  40.1 us (7%)
  other arithmetic  33 us (6%)
  starting transfers between devices  28.9 us (5%)
  between operations  15.3 us (3%)
    all_to_all x1, waiting for transfers between devices, on_device(): right_all = jnp.concatenate(lax.all_to_all(repeated, 'row', 0, 0), axis=0)  88.8 us
    reduce_scatter x1, waiting for transfers between devices, on_device(): lax.psum_scatter(jnp.einsum('jkc,ikc->jic', right_all, left_side, preferr...  83.4 us
    all_gather x1, waiting for transfers between devices, gathered_total(): return lax.all_gather(array, axis).sum(0)  65.2 us
    all_to_all x2, waiting for transfers between devices, sent_and_summed(): blocks = lax.all_to_all(split_up(array, dim, size), axis, 0, 0, tiled=True)  48 us
    all_to_all x2, blocking collectives, sent_to_all(): return lax.all_to_all(copies, axis, split_axis=0, concat_axis=0, tiled=True)  31.5 us
    unnamed x87, local copies, waits for them, and re-layouts  30.7 us
    all_to_all x1, waiting for transfers between devices, sent_to_all(): return lax.all_to_all(copies, axis, split_axis=0, concat_axis=0, tiled=True)  17.2 us
    transpose x1, local copies, waits for them, and re-layouts, on_device(): jnp.einsum('jkc,ikc->jic', right_all, left_side, preferred_element_type=j...  16.8 us
  transfers between devices with their start and end apart: 7, of which 7 were waited for; matrix products, arithmetic and copies ran while one was open for 5% of the time, Pallas kernels for 0%

profile of v1, /device:TPU:32, one launch (start us, length us, event | category | flops | bytes accessed | tf_op | source)
XLA Modules:
  0.0 551.9 jit_solution(4047227765900731330)
XLA Ops:
  11.2 1.8 fusion.118
  15.8 1.7 copy-done.1
  17.5 2.7 stack.4
  20.2 6.2 %all-to-all-start = ((bf16[8,64,32,128]{3,2,1,0:T(8,128)(2,1)}), bf16[8,64,32,128]{3,2,1,0:T(8,128)(2,1)}, u32[]{:S(2)}, u32[]{:S(2)}) async-start(bf16[8,64,32,128]{3,2,1,0:T(8,128)(2,1)} %stack.4), calls=%async_computation | async-start | bytes 8388608 | tf_op jit(solution)/shard_map/all_to_all | solution.py:125
  26.4 1.7 copy.132
  28.2 88.8 %all-to-all-done = bf16[8,64,32,128]{3,2,1,0:T(8,128)(2,1)} async-done(((bf16[8,64,32,128]{3,2,1,0:T(8,128)(2,1)}), bf16[8,64,32,128]{3,2,1,0:T(8,128)(2,1)}, u32[]{:S(2)}, u32[]{:S(2)}) %all-to-all-start) | async-done | bytes 4194336 | tf_op jit(solution)/shard_map/all_to_all | solution.py:125
  117.0 8.6 %copy.133 = bf16[512,32,128]{0,1,2:T(8,128)(2,1)} copy(bf16[512,32,128]{2,1,0:T(8,128)(2,1)} %bitcast.2) | data formatting | bytes 8388608 | tf_op jit(solution)/shard_map/reshape | solution.py:125
  125.6 10.3 %convolution_bitcast_fusion = f32[512,64,128]{0,1,2:T(8,128)} fusion(bf16[64,32,128]{0,1,2:T(8,128)(2,1)S(1)} %copy.132, bf16[512,32,128]{0,1,2:T(8,128)(2,1)} %copy.133), kind=kOutput, calls=%fused_computation.2 | convolution fusion | flops 268435456 | bytes 21495808 | tf_op jit(solution)/shard_map/jkc,ikc->jic/dot_general | solution.py:128
  135.8 16.8 %copy.134 = f32[512,64,128]{2,1,0:T(8,128)} copy(f32[512,64,128]{0,1,2:T(8,128)} %convolution_bitcast_fusion) | data formatting | bytes 33554432 | tf_op jit(solution)/shard_map/jkc,ikc->jic/transpose | solution.py:128
  154.4 2.0 fusion.82
  159.7 2.0 reshape.273
  161.7 8.3 %all-to-all-start.1 = ((bf16[8,2,24576]{2,1,0:T(2,128)(2,1)}), bf16[8,2,24576]{2,1,0:T(2,128)(2,1)}, u32[]{:S(2)}, u32[]{:S(2)}) async-start(bf16[8,2,24576]{2,1,0:T(2,128)(2,1)} %reshape.273), calls=%async_computation.2 | async-start | bytes 1572864 | tf_op jit(solution)/shard_map/all_to_all | solution.py:20
  170.1 17.2 %all-to-all-done.1 = bf16[8,2,24576]{2,1,0:T(2,128)(2,1)} async-done(((bf16[8,2,24576]{2,1,0:T(2,128)(2,1)}), bf16[8,2,24576]{2,1,0:T(2,128)(2,1)}, u32[]{:S(2)}, u32[]{:S(2)}) %all-to-all-start.1) | async-done | bytes 786464 | tf_op jit(solution)/shard_map/all_to_all | solution.py:20
  187.4 2.2 reshape.274
  189.6 83.4 %reduce-scatter.2.cloned.1.call-done = f32[32,64,128]{2,1,0:T(8,128)} async-done(((f32[512,64,128]{2,1,0:T(8,128)}), f32[32,64,128]{2,1,0:T(8,128)}) %reduce-scatter.2.cloned.1.call-update) | async-done | bytes 1048592 | tf_op jit(solution)/shard_map/reduce_scatter | solution.py:127
  273.0 1.7 bitcast_reduce_fusion.1
  276.0 1.8 fusion.17
  280.5 4.9 all-to-all-start.2
  287.5 5.5 %all-to-all-done.2 = bf16[16,2,1024]{2,1,0:T(2,128)(2,1)S(1)} async-done(((bf16[16,2,1024]{2,1,0:T(2,128)(2,1)}), bf16[16,2,1024]{2,1,0:T(2,128)(2,1)S(1)}, u32[]{:S(2)}, u32[]{:S(2)}) %all-to-all-start.2) | async-done | bytes 65568 | tf_op jit(solution)/shard_map/all_to_all | solution.py:144
  293.3 1.5 fusion.119
  295.8 2.5 convolution_bitcast_fusion.1
  298.3 2.2 copy.172
  300.5 2.9 reshape.277
  303.4 3.9 all-to-all-start.3
  310.1 19.4 %all-to-all-done.3 = f32[16,1,24576]{2,1,0:T(1,128)S(1)} async-done(((f32[16,1,24576]{2,1,0:T(1,128)}), f32[16,1,24576]{2,1,0:T(1,128)S(1)}, u32[]{:S(2)}, u32[]{:S(2)}) %all-to-all-start.3) | async-done | bytes 1572896 | tf_op jit(solution)/shard_map/all_to_all | solution.py:35
  330.1 6.2 %reduce.12 = f32[16,24576]{1,0:T(8,128)} reduce(f32[16,1,24576]{2,1,0:T(1,128)S(1)} %all-to-all-done.3, f32[]{:T(128)} %broadcast.249), dimensions={1}, to_apply=%all_to_all.41.reduce_sub_computation | reduce | bytes 3145732 | tf_op jit(solution)/shard_map/all_to_all | solution.py:35
  336.2 2.4 reshape.278
  342.4 16.6 %all_to_all.57 = bf16[16,2,12288]{2,1,0:T(2,128)(2,1)S(1)} all-to-all(bf16[16,2,12288]{2,1,0:T(2,128)(2,1)S(1)} %reshape.279), channel_id=1, replica_groups=mesh['row'=8,'col'=16,'samp'=2] {'col'}, dimensions={0} | all-to-all | bytes 1572864 | tf_op jit(solution)/shard_map/all_to_all | solution.py:20
  361.3 3.5 copy.144
  364.8 2.5 reshape.257
  370.1 4.4 convolution_bitcast_fusion.3
  374.5 2.6 pad_maximum_fusion
  377.1 2.4 reshape.258
  379.5 2.2 copy.171
  381.8 4.8 reshape.283
  386.6 5.4 all-to-all-start.7
  392.3 5.4 fusion.20
  397.7 28.6 %all-to-all-done.7 = f32[8,1,49152]{2,1,0:T(1,128)S(1)} async-done(((f32[8,1,49152]{2,1,0:T(1,128)}), f32[8,1,49152]{2,1,0:T(1,128)S(1)}, u32[]{:S(2)}, u32[]{:S(2)}) %all-to-all-start.7) | async-done | bytes 1572896 | tf_op jit(solution)/shard_map/all_to_all | solution.py:35
  426.3 6.3 %reduce.15 = f32[8,49152]{1,0:T(8,128)} reduce(f32[8,1,49152]{2,1,0:T(1,128)S(1)} %all-to-all-done.7, f32[]{:T(128)} %broadcast.249), dimensions={1}, to_apply=%all_to_all.48.reduce_sub_computation | reduce | bytes 3145732 | tf_op jit(solution)/shard_map/all_to_all | solution.py:35
  432.6 2.7 reshape.284
  437.9 1.6 fusion.42
  441.2 2.8 fusion.120
  444.0 14.9 %all_to_all.58 = f32[2,1,64,512]{3,2,1,0:T(8,128)S(1)} all-to-all(f32[2,1,64,512]{3,2,1,0:T(8,128)S(1)} %broadcast_in_dim.23), channel_id=1, replica_groups=mesh['row'=8,'col'=16,'samp'=2] {'samp'}, dimensions={0} | all-to-all | bytes 524288 | tf_op jit(solution)/shard_map/all_to_all | solution.py:20
  459.0 1.3 reduce.13
  460.6 11.2 %all_to_all.59 = f32[16,1,2048]{2,1,0:T(1,128)S(1)} all-to-all(f32[16,1,2048]{2,1,0:T(1,128)S(1)} %reshape.281), channel_id=1, replica_groups=mesh['row'=8,'col'=16,'samp'=2] {'col'}, dimensions={0} | all-to-all | bytes 262144 | tf_op jit(solution)/shard_map/all_to_all | solution.py:222
  473.4 2.0 fusion.45
  475.4 65.2 %all-gather.3.cloned.1.call-done = f32[2048,384]{1,0:T(8,128)} async-done(((f32[64,384]{1,0:T(8,128)}), f32[2048,384]{1,0:T(8,128)}) %all-gather.3.cloned.1.call-update) | async-done | bytes 3145744 | tf_op jit(solution)/shard_map/all_gather | solution.py:40
  540.6 2.2 reduce_sum.208
  (152 shorter events, 39.6 us)
Async XLA Ops:
  7.2 150.8 %copy-start = (bf16[768,3,48]{0,2,1:T(8,128)(2,1)S(1)}, bf16[768,3,48]{0,2,1:T(8,128)(2,1)}, u32[]{:S(2)}) copy-start(bf16[768,3,48]{0,2,1:T(8,128)(2,1)} %param.25) | copy-start | bytes 663556
  7.2 6.9 %copy-start.19 = (bf16[128,640]{1,0:T(8,128)(2,1)S(1)}, bf16[128,640]{1,0:T(8,128)(2,1)}, u32[]{:S(2)}) copy-start(bf16[128,640]{1,0:T(8,128)(2,1)} %param.19) | copy-start | bytes 491524
  15.1 2.4 copy-start.1
  20.2 96.8 %all-to-all-start = ((bf16[8,64,32,128]{3,2,1,0:T(8,128)(2,1)}), bf16[8,64,32,128]{3,2,1,0:T(8,128)(2,1)}, u32[]{:S(2)}, u32[]{:S(2)}) async-start(bf16[8,64,32,128]{3,2,1,0:T(8,128)(2,1)} %stack.4), calls=%async_computation | async-start | bytes 8388608 | tf_op jit(solution)/shard_map/all_to_all | solution.py:125
  26.4 246.5 %reduce-scatter.2.cloned.1.call-start = ((), (), s32[]{:S(2)}) async-start(), calls=%async_computation.9 | async-start | bytes 17825792 | tf_op jit(solution)/shard_map/reduce_scatter | solution.py:127
  152.6 0.8 copy-start.10
  152.6 1.2 copy-start.4
  153.5 2.8 copy-start.25
  154.3 3.6 copy-start.28
  154.4 3.6 copy-start.30
  156.4 0.8 copy-start.9
  158.7 0.7 copy-start.20
  159.7 10.3 %copy-start.17 = (bf16[48,768]{1,0:T(8,128)(2,1)S(1)}, bf16[48,768]{1,0:T(8,128)(2,1)}, u32[]{:S(2)}) copy-start(bf16[48,768]{1,0:T(8,128)(2,1)} %param.26) | copy-start | bytes 221188
  159.7 10.4 %copy-start.27 = (s32[512]{0:T(512)S(1)}, s32[512]{0:T(512)}, u32[]{:S(2)}) copy-start(s32[512]{0:T(512)} %param.17) | copy-start | bytes 6148
  161.7 25.7 %all-to-all-start.1 = ((bf16[8,2,24576]{2,1,0:T(2,128)(2,1)}), bf16[8,2,24576]{2,1,0:T(2,128)(2,1)}, u32[]{:S(2)}, u32[]{:S(2)}) async-start(bf16[8,2,24576]{2,1,0:T(2,128)(2,1)} %reshape.273), calls=%async_computation.2 | async-start | bytes 1572864 | tf_op jit(solution)/shard_map/all_to_all | solution.py:20
  273.0 1.7 copy-start.3
  274.6 1.3 copy-start.34
  276.0 2.7 copy-start.24
  277.8 0.8 copy-start.16
  280.5 12.5 %all-to-all-start.2 = ((bf16[16,2,1024]{2,1,0:T(2,128)(2,1)}), bf16[16,2,1024]{2,1,0:T(2,128)(2,1)S(1)}, u32[]{:S(2)}, u32[]{:S(2)}) async-start(bf16[16,2,1024]{2,1,0:T(2,128)(2,1)} %reshape.275), calls=%async_computation.3 | async-start | bytes 131072 | tf_op jit(solution)/shard_map/all_to_all | solution.py:144
  287.4 7.3 %copy-start.7 = (bf16[8,512,2,48]{1,3,0,2:T(8,128)(2,1)}, bf16[8,512,2,48]{1,3,0,2:T(8,128)(2,1)S(1)}, u32[]{:S(2)}) copy-start(bf16[8,512,2,48]{1,3,0,2:T(8,128)(2,1)S(1)} %reshape.252) | copy-start | bytes 2359300
  294.8 1.0 copy-start.13
  294.8 1.0 copy-start.32
  303.4 26.1 %all-to-all-start.3 = ((f32[16,1,24576]{2,1,0:T(1,128)}), f32[16,1,24576]{2,1,0:T(1,128)S(1)}, u32[]{:S(2)}, u32[]{:S(2)}) async-start(f32[16,1,24576]{2,1,0:T(1,128)} %reshape.277), calls=%async_computation.4 | async-start | bytes 3145728 | tf_op jit(solution)/shard_map/all_to_all | solution.py:35
  338.6 0.7 copy-start.22
  338.7 0.9 copy-start.23
  364.8 2.5 copy-start.18
  367.3 1.8 copy-start.14
  367.3 1.8 copy-start.33
  369.2 1.0 copy-start.11
  386.5 5.7 %copy-start.21 = (f32[64,48]{0,1:T(8,128)S(1)}, f32[64,48]{0,1:T(8,128)}, u32[]{:S(2)}) copy-start(f32[64,48]{0,1:T(8,128)} %get-tuple-element.11) | copy-start | bytes 36868
  386.5 5.7 %copy-start.8 = (bf16[8,512,2,48]{1,3,0,2:T(8,128)(2,1)S(1)}, bf16[8,512,2,48]{1,3,0,2:T(8,128)(2,1)}, u32[]{:S(2)}) copy-start(bf16[8,512,2,48]{1,3,0,2:T(8,128)(2,1)} %copy-done.7) | copy-start | bytes 2359300
  386.6 39.8 %all-to-all-start.7 = ((f32[8,1,49152]{2,1,0:T(1,128)}), f32[8,1,49152]{2,1,0:T(1,128)S(1)}, u32[]{:S(2)}, u32[]{:S(2)}) async-start(f32[8,1,49152]{2,1,0:T(1,128)} %reshape.283), calls=%async_computation.8 | async-start | bytes 3145728 | tf_op jit(solution)/shard_map/all_to_all | solution.py:35
  392.0 148.6 %all-gather.3.cloned.1.call-start = ((), (), s32[]{:S(2)}) async-start(), calls=%async_computation.10 | async-start | bytes 3244032 | tf_op jit(solution)/shard_map/all_gather | solution.py:40
  435.3 1.1 copy-start.5
  435.3 1.1 copy-start.31
  435.3 1.1 copy-start.35
  436.4 1.5 copy-start.6
  437.0 4.2 copy-start.12
  437.0 4.2 copy-start.15
  540.6 2.2 copy-start.26
  540.6 2.2 copy-start.29
  540.6 2.8 copy-start.2
Sparse Core Ops, SparseCore 0:
  152.8 120.1 reduce-scatter.1
  441.3 99.2 all-gather.2
